TPU v7x, 128 devices: a whole 4x4x4 slice. The times are simulated.
128 devices in a mesh: req: 16 (over y, x), seq: 4 (over z), hid: 2 (over core).
Axes of the slice: x: 4, y: 4, z: 4, core: 2. Of those that a mesh axis runs over, the one named last changes fastest.
Arguments:
- tokens: bfloat16 [65536, 2048], P(('req', 'seq')), may hold values from -6 to 6
- attention_gain: bfloat16 [2048], replicated, may hold values from 0.099609375 to 1.8984375
- project_weight: bfloat16 [2048, 2048], P(None, 'hid'), may hold values from -0.125 to 0.125
- conv_weight: bfloat16 [4, 2048], P(None, 'hid'), may hold values from -3 to 3
- decay_down: bfloat16 [2048, 16], replicated, may hold values from -0.125 to 0.125
- decay_up: bfloat16 [16, 512], P(None, 'hid'), may hold values from -1.5 to 1.5
- decay_bias: float32 [512], P('hid'), may hold values from -2 to 10
- output_gate: bfloat16 [2048, 1024], P(None, 'hid'), may hold values from -0.125 to 0.125
- head_gain: bfloat16 [512], replicated, may hold values from 0.099609375 to 1.8984375
- output_weight: bfloat16 [1024, 2048], P('hid'), may hold values from -0.1875 to 0.1875
- mixer_gain: bfloat16 [2048], replicated, may hold values from 0.099609375 to 1.8984375
- gate_weight: bfloat16 [2048, 2816], P('req', 'hid'), may hold values from -0.125 to 0.125
- up_weight: bfloat16 [2048, 2816], P('req', 'hid'), may hold values from -0.125 to 0.125
- down_weight: bfloat16 [2816, 2048], P('hid', 'req'), may hold values from -0.109375 to 0.109375
- prompt_pages: int32 [16, 16], P('req'), may hold values from 0 to 64, as said below
- prompt_start: int32 [16, 16], P('req'), may hold values from 0 to 63, as said below
Outputs:
- hidden_out: bfloat16 [65536, 2048], P(('req', 'seq', 'hid'))
- page_states: bfloat16 [1024, 2, 256, 512], P(('req', 'seq'), 'hid')
- conv_edges: bfloat16 [1024, 3, 2048], P(('req', 'seq'), None, 'hid')
Inputs may be any that keep to these rules, and one draw needn't show every extreme that they name: `prompt_pages`: row r lists the page counts of the prompts of group r; 0 marks an unused slot; in every draw some group holds one prompt of all its 64 pages. `prompt_start`: the slots of a row that are used cover pages in increasing order without intersection and end by page 64; pages between prompts belong to none; an unused slot starts at page 64 - 1, and every draw has one.
All inputs are finite; a program needn't handle non-finite values.
Results may differ from a plain program's by a relative error of at most 0.014.
Values may be sent and summed in bfloat16 or wider, within the bound.
A program may use at most 192 MiB of HBM per device.

v0:
```python
import jax
import jax.numpy as jnp
from jax import lax
from jax.sharding import PartitionSpec as P

HK = 256
HV = 512
KCONV = 4
PAGE = 64
CONVW = 1024
EPSILON = 1e-06
TOP_PRECISION = lax.Precision.HIGHEST


def shifted(value, axis, steps):
    count = lax.axis_size(axis)
    first, last = (max(0, -steps), min(count, count - steps))
    return lax.ppermute(value, axis, [(source, source + steps) for source in range(first, last)])


def prefix_2(array, axis, join, neutral):
    place = lax.axis_index(axis)
    gathered = jax.tree.map(
        lambda a, kind: lax.all_gather(a.astype(kind), axis), array, (jnp.bfloat16, jnp.bfloat16)
    )
    state = jax.tree.map(lambda a, e: jnp.zeros_like(a) + jnp.asarray(e, a.dtype), array, neutral)

    def one(lap, state):
        return join(
            state,
            jax.tree.map(
                lambda a, own: lax.dynamic_index_in_dim(a, lap, 0, False).astype(own.dtype),
                gathered,
                array,
            ),
        )

    return lax.fori_loop(0, place, one, state)


def rms_scaled(values, scale_gain):
    values = values.astype(jnp.float32)
    return (
        values
        * lax.rsqrt(jnp.mean(values * values, axis=-1, keepdims=True) + EPSILON)
        * scale_gain.astype(jnp.float32)
    )


def page_segments(page_counts, starts, total_pages):
    position = jnp.arange(total_pages, dtype=jnp.int32)
    inside = (position[None, :] >= starts[:, None]) & (
        position[None, :] < starts[:, None] + page_counts[:, None]
    )
    labels = jnp.arange(1, page_counts.shape[0] + 1, dtype=jnp.int32)
    segment = jnp.sum(jnp.where(inside, labels[:, None], 0), axis=0) - 1
    earlier = jnp.concatenate([jnp.full((1,), -1, jnp.int32), segment[:-1]])
    return ((segment == earlier) & (segment >= 0)).astype(jnp.float32)


def short_conv(by_page, before, carried, conv_taps):
    kept_rows = before.astype(jnp.float32) * carried[:, None, None]
    widened = jnp.concatenate([kept_rows, by_page.astype(jnp.float32)], axis=1)
    tap_count = conv_taps.shape[0]
    length = by_page.shape[1]
    result = jnp.zeros(by_page.shape, jnp.float32)
    for offset in range(tap_count):
        result = (
            result
            + conv_taps[offset].astype(jnp.float32)
            * widened[:, tap_count - 1 - offset : tap_count - 1 - offset + length]
        )
    return result


def split_features(mixed_rows, key_width):
    query_rows = jax.nn.silu(mixed_rows[..., :key_width])
    key_rows = jax.nn.silu(mixed_rows[..., key_width : 2 * key_width]) * key_width ** (-0.5)
    value_matrix = mixed_rows[..., 2 * key_width :]
    return (
        query_rows.transpose(0, 2, 1, 3),
        key_rows.transpose(0, 2, 1, 3),
        value_matrix.transpose(0, 2, 1, 3),
    )


def page_step(memory_state, inputs):
    query_rows, key_rows, value_matrix, decay_sum, carried = inputs
    memory_state = memory_state * carried
    length = query_rows.shape[1]
    raised_rows = query_rows * jnp.exp(decay_sum)
    lowered = key_rows * jnp.exp(-decay_sum)
    scores = jnp.einsum("hik,hjk->hij", raised_rows, lowered, precision=TOP_PRECISION)
    rows_index = jnp.arange(length)
    causal = rows_index[:, None] >= rows_index[None, :]
    scores = jnp.where(causal[None], scores, 0.0)
    layer_output = jnp.einsum("hij,hjv->hiv", scores, value_matrix, precision=TOP_PRECISION)
    layer_output = layer_output + jnp.einsum(
        "eow,ews->eos", raised_rows, memory_state, precision=TOP_PRECISION
    )
    closing_sum = decay_sum[:, -1:, :]
    weighted_rows = key_rows * jnp.exp(closing_sum - decay_sum)
    memory_state = jnp.exp(closing_sum[:, 0, :])[:, :, None] * memory_state + jnp.einsum(
        "lte,ltb->leb", weighted_rows, value_matrix, precision=TOP_PRECISION
    )
    return (memory_state, (layer_output, memory_state))


def on_device(
    tokens,
    attention_gain,
    project_weight,
    conv_weight,
    decay_down,
    decay_up,
    decay_bias,
    output_gate,
    head_gain,
    output_weight,
    mixer_gain,
    gate_weight,
    up_weight,
    down_weight,
    prompt_pages,
    prompt_start,
):
    token_count = tokens.shape[0]
    page_count = token_count // PAGE
    local_heads = project_weight.shape[1] // CONVW
    rim_rows = KCONV - 1
    seq_index = lax.axis_index("seq")
    group_pages = page_count * lax.axis_size("seq")
    page_flags = page_segments(prompt_pages[0], prompt_start[0], group_pages)
    carried = lax.dynamic_slice_in_dim(page_flags, seq_index * page_count, page_count)
    normed = rms_scaled(tokens, attention_gain).astype(jnp.bfloat16)
    projected = jnp.dot(normed, project_weight, preferred_element_type=jnp.float32).astype(
        jnp.bfloat16
    )
    by_page = projected.reshape(page_count, PAGE, local_heads * CONVW)
    incoming = shifted(by_page[-1, PAGE - rim_rows :], "seq", 1)
    before = jnp.concatenate([incoming[None], by_page[:-1, PAGE - rim_rows :]], axis=0)
    mixed_rows = short_conv(by_page, before, carried, conv_weight).reshape(
        page_count, PAGE, local_heads, CONVW
    )
    query_rows, key_rows, value_matrix = split_features(mixed_rows, HK)
    lowrank = jnp.dot(normed, decay_down, preferred_element_type=jnp.float32).astype(jnp.bfloat16)
    decay_log = (
        jax.nn.log_sigmoid(
            jnp.dot(lowrank, decay_up, preferred_element_type=jnp.float32) + decay_bias
        )
        / 16.0
    )
    decay_log = decay_log.reshape(page_count, PAGE, local_heads, HK).transpose(0, 2, 1, 3)
    decay_sum = jnp.cumsum(decay_log, axis=2)
    start_memory = jnp.zeros((local_heads, HK, HV), jnp.float32)
    local_memory, (outputs, memories) = lax.scan(
        page_step, start_memory, (query_rows, key_rows, value_matrix, decay_sum, carried)
    )
    totals = decay_sum[:, :, -1, :]
    through = jnp.cumsum(totals, axis=0)
    alive_mask = jnp.cumprod(carried)
    block_decay = alive_mask[-1] * jnp.exp(through[-1])

    def compose(earlier, latter):
        return (earlier[0] * latter[0], latter[0][..., None] * earlier[1] + latter[1])

    prefix = prefix_2(
        (block_decay, local_memory),
        "seq",
        compose,
        (jnp.ones_like(block_decay), jnp.zeros_like(local_memory)),
    )
    incoming_state = prefix[1]
    before_sum = through - totals
    extent_factor = alive_mask[:, None, None, None] * jnp.exp(decay_sum + before_sum[:, :, None, :])
    outputs = outputs + jnp.einsum(
        "dlof,lfg->dlog", query_rows * extent_factor, incoming_state, precision=TOP_PRECISION
    )
    memories = (
        memories + (alive_mask[:, None, None] * jnp.exp(through))[..., None] * incoming_state[None]
    )
    attended = outputs.transpose(0, 2, 1, 3).reshape(token_count, local_heads, HV)
    normed_heads = rms_scaled(attended, head_gain)
    opening = jax.nn.silu(jnp.dot(normed, output_gate, preferred_element_type=jnp.float32)).reshape(
        token_count, local_heads, HV
    )
    gated_rows = (
        (normed_heads * opening).astype(jnp.bfloat16).reshape(token_count, local_heads * HV)
    )
    partial_value = jnp.dot(gated_rows, output_weight, preferred_element_type=jnp.float32)
    half_rows = token_count // lax.axis_size("hid")
    row_start = lax.axis_index("hid") * half_rows
    mixed_sum = lax.psum(partial_value.astype(jnp.bfloat16), "hid").astype(jnp.float32)
    residual = (tokens.astype(jnp.float32) + mixed_sum).astype(jnp.bfloat16)
    feed_in = rms_scaled(residual, mixer_gain).astype(jnp.bfloat16)
    own_residual = lax.dynamic_slice_in_dim(residual, row_start, half_rows, 0)

    def widen(weight_rows):
        return jnp.dot(feed_in, weight_rows, preferred_element_type=jnp.float32)

    gate_part = widen(lax.all_gather(gate_weight, "req", axis=0, tiled=True))
    up_part = widen(lax.all_gather(up_weight, "req", axis=0, tiled=True))
    hidden = (jax.nn.silu(gate_part) * up_part).astype(jnp.bfloat16)
    partials = jnp.dot(
        hidden,
        lax.all_gather(down_weight, "req", axis=1, tiled=True),
        preferred_element_type=jnp.float32,
    )
    feed_sum = lax.psum_scatter(
        partials.astype(jnp.bfloat16), "hid", scatter_dimension=0, tiled=True
    ).astype(jnp.float32)
    result = (own_residual.astype(jnp.float32) + feed_sum).astype(jnp.bfloat16)
    return (result, memories.astype(jnp.bfloat16), by_page[:, PAGE - rim_rows :])


def solution(mesh):
    return jax.shard_map(
        on_device,
        mesh=mesh,
        in_specs=(
            P(("req", "seq"), None),
            P(),
            P(None, "hid"),
            P(None, "hid"),
            P(),
            P(None, "hid"),
            P("hid"),
            P(None, "hid"),
            P(),
            P("hid", None),
            P(),
            P("req", "hid"),
            P("req", "hid"),
            P("hid", "req"),
            P("req", None),
            P("req", None),
        ),
        out_specs=(
            P(("req", "seq", "hid"), None),
            P(("req", "seq"), "hid", None, None),
            P(("req", "seq"), None, "hid"),
        ),
        check_vma=False,
    )
```

profile of v0, /device:TPU:1, one launch (start us, length us, event | category | flops | bytes accessed | tf_op | source)
XLA Modules:
  0.0 471.6 jit_solution(12928191912061938082)
XLA Ops:
  8.1 3.2 fusion.29
  11.6 7.2 %convolution_convert_fusion.2 = bf16[1024,1024]{1,0:T(8,128)(2,1)S(1)} fusion(bf16[2048,1024]{1,0:T(8,128)(2,1)} %param.22, bf16[1024,2048]{1,0:T(8,128)(2,1)S(1)} %copy-done.2, f32[2048]{0:T(1024)S(1)} %convert_element_type.146, f32[1024]{0:T(1024)S(1)} %add_rsqrt_fusion.2), kind=kOutput, calls=%fused_computation.78 | convolution fusion | flops 4304404480 | bytes 10498048 | tf_op jit(solution)/shard_map/dot_general | solution.py:136
  18.9 4.5 collective-permute-start
  23.5 3.2 copy_convert_fusion
  26.9 4.2 fusion.50
  34.4 7.3 %fusion.37 = f32[16,64,1,1024]{3,0,1,2:T(8,128)S(1)} fusion(f32[16,64,1024]{2,0,1:T(8,128)} %copy_convert_fusion, f32[16,3,1024]{2,0,1:T(8,128)S(1)} %convert_multiply_fusion.4, f32[1024]{0:T(1024)S(1)} %bitcast.168, f32[1024]{0:T(1024)S(1)} %bitcast.169, f32[1024]{0:T(1024)S(1)} %bitcast.167, f32[1024]{0:T(1024)S(1)} %bitcast.166), kind=kLoop, calls=%fused_computation.61 | loop fusion | flops 10485760 | bytes 8601600 | tf_op jit(solution)/shard_map/reshape | solution.py:142
  45.4 143.3 %while.28 = (s32[]{:T(128)}, f32[1,256,512]{2,1,0:T(8,128)S(1)}, f32[16,1,64,512]{3,2,1,0:T(8,128)}, f32[16,1,256,512]{3,2,1,0:T(8,128)}, f32[16,1,64,256]{3,0,1...) while((s32[]{:T(128)}, f32[1,256,512]{2,1,0:T(8,128)S(1)}, ...), condition=%wide.region_4.5_spmd.clone, body=%wide.region_3.4_spmd.clone.sunk | while | flops 240001024 | bytes 4038800 | solution.py:156
  70.1 2.2 bitcast_dynamic-update-slice_fusion.2
  141.7 2.2 bitcast_dynamic-update-slice_fusion.2
  190.8 6.9 %all_gather.19 = bf16[4,1,256]{2,1,0:T(2,128)(2,1)S(1)} all-gather(bf16[1,1,256]{2,1,0:T(2,128)(2,1)S(1)} %fusion.65), channel_id=1, replica_groups=mesh['req'=16,'seq'=4,'hid'=2] {'seq'}, dimensions={0}, use_global_device_ids=true | all-gather | bytes 2560 | tf_op jit(solution)/shard_map/all_gather | solution.py:24
  197.7 17.4 %all-gather.12.cloned.1.call-done = bf16[4,256,512]{2,1,0:T(8,128)(2,1)} async-done(((bf16[1,256,512]{2,1,0:T(8,128)(2,1)}), bf16[4,256,512]{2,1,0:T(8,128)(2,1)}) %all-gather.12.cloned.1.call-update) | async-done | bytes 1048592 | tf_op jit(solution)/shard_map/all_gather | solution.py:24
  215.4 5.6 %multiply_reduce_fusion = (f32[16,64]{1,0:T(8,128)S(1)}, f32[16,1,64,512]{3,2,0,1:T(8,128)}) fusion(f32[16,64,256]{2,0,1:T(8,128)} %get-tuple-element.223, f32[1,256,512]{2,1,0:T(8,128)S(1)} %get-tuple-element.98, f32[16,1,64,512]{3,2,1,0:T(8,128)} %get-tuple-element.96), kind=kOutput, calls=%fused_computation.77 | convolution fusion | flops 1612184576 | bytes 5771264 | tf_op jit(solution)/shard_map/dlof,lfg->dlog/dot_general | solution.py:176
  221.1 6.2 %fusion.44 = bf16[1024,512]{1,0:T(8,128)(2,1)S(1)} fusion(f32[16,1,64,512]{3,2,0,1:T(8,128)} %get-tuple-element.231, f32[512]{0:T(512)S(1)} %convert_element_type.163, f32[1024]{0:T(1024)S(1)} %rsqrt.29, bf16[2048,512]{1,0:T(8,128)(2,1)} %param.27, bf16[1024,2048]{1,0:T(8,128)(2,1)} %param.20, f32[2048]{0:T(1024)S(1)} %convert_element_type.146, ...), kind=kOutput, calls=%fused_computation.76 | convolution fusion | flops 2160066560 | bytes 9455616 | tf_op jit(solution)/shard_map/dot_general | solution.py:184
  227.2 4.4 convolution_convert_fusion.1
  233.7 36.6 %all-reduce.2.cloned.1.call-done = bf16[1024,2048]{1,0:T(8,128)(2,1)} async-done(((bf16[1024,2048]{1,0:T(8,128)(2,1)}), bf16[1024,2048]{1,0:T(8,128)(2,1)}) %all-reduce.2.cloned.1.call-update) | async-done | bytes 4194320 | tf_op jit(solution)/shard_map/psum | solution.py:193
  270.3 7.7 %fusion.26 = (f32[1024]{0:T(1024)S(1)}, bf16[1024,2048]{1,0:T(8,128)(2,1)}) fusion(bf16[1024,2048]{1,0:T(8,128)(2,1)} %all-reduce.2.cloned.1.call-done, bf16[1024,2048]{1,0:T(8,128)(2,1)} %param.20), kind=kLoop, calls=%fused_computation.44 | loop fusion | flops 14679040 | bytes 12587008 | tf_op jit(solution)/shard_map/reduce_sum | solution.py:45
  278.0 19.1 %all-gather.6.cloned.1.call-done = bf16[2048,1408]{1,0:T(8,128)(2,1)} async-done(((bf16[128,1408]{1,0:T(8,128)(2,1)}), bf16[2048,1408]{1,0:T(8,128)(2,1)}) %all-gather.6.cloned.1.call-update) | async-done | bytes 5767184 | tf_op jit(solution)/shard_map/all_gather | solution.py:201
  297.1 12.0 %fusion.47 = f32[1024,1408]{1,0:T(8,128)} fusion(bf16[2048,1408]{1,0:T(8,128)(2,1)} %all-gather.6.cloned.1.call-done, bf16[1024,2048]{1,0:T(8,128)(2,1)} %get-tuple-element.218, f32[2048]{0:T(1024)S(1)} %convert_element_type.170, f32[1024]{0:T(1024)S(1)} %add_rsqrt_fusion.1), kind=kOutput, calls=%fused_computation.81 | convolution fusion | flops 5913968640 | bytes 15740928 | tf_op jit(solution)/shard_map/dot_general | solution.py:199
  309.0 53.5 %all-gather.10.cloned.1.call-done = bf16[1408,2048]{1,0:T(8,128)(2,1)} async-done(((bf16[1408,128]{1,0:T(8,128)(2,1)}), bf16[1408,2048]{1,0:T(8,128)(2,1)}) %all-gather.10.cloned.1.call-update) | async-done | bytes 5767184 | tf_op jit(solution)/shard_map/all_gather | solution.py:206
  362.5 61.3 %all-gather.8.cloned.1.call-done = bf16[2048,1408]{1,0:T(8,128)(2,1)} async-done(((bf16[128,1408]{1,0:T(8,128)(2,1)}), bf16[2048,1408]{1,0:T(8,128)(2,1)}) %all-gather.8.cloned.1.call-update) | async-done | bytes 5767184 | tf_op jit(solution)/shard_map/all_gather | solution.py:202
  423.8 20.9 %convolution_convert_fusion = bf16[1024,2048]{1,0:T(8,128)(2,1)} fusion(bf16[1408,2048]{1,0:T(8,128)(2,1)} %all-gather.10.cloned.1.call-done, f32[1024,1408]{1,0:T(8,128)} %fusion.47, bf16[2048,1408]{1,0:T(8,128)(2,1)} %all-gather.8.cloned.1.call-done, bf16[1024,2048]{1,0:T(8,128)(2,1)} %get-tuple-element.218, f32[2048]{0:T(1024)S(1)} %convert_element_type.170, ...), kind=kOutput, calls=%fused_computation.68 | convolution fusion | flops 11830296576 | bytes 25702400 | tf_op jit(solution)/shard_map/dot_general | solution.py:204
  446.5 5.4 %add_convert_fusion = bf16[16,1,256,512]{3,2,1,0:T(8,128)(2,1)} fusion(f32[16,1,256,512]{3,2,1,0:T(8,128)} %get-tuple-element.99, f32[256,512]{1,0:T(8,128)S(1)} %bitcast.155, f32[16,256]{1,0:T(8,128)S(1)} %bitcast_multiply_fusion.1), kind=kLoop, calls=%fused_computation.51 | loop fusion | flops 6291456 | bytes 13123584 | tf_op jit(solution)/shard_map/convert_element_type | solution.py:213
  451.8 7.9 %reduce-scatter.2.cloned.1.call-done = bf16[512,2048]{1,0:T(8,128)(2,1)} async-done(((bf16[1024,2048]{1,0:T(8,128)(2,1)}), bf16[512,2048]{1,0:T(8,128)(2,1)}) %reduce-scatter.2.cloned.1.call-update) | async-done | bytes 2097168 | tf_op jit(solution)/shard_map/reduce_scatter | solution.py:209
  459.8 4.4 add_convert_fusion.1
  (256 shorter events, 152.0 us)
Async XLA Ops:
  8.0 219.2 %copy-start = (bf16[512,2048]{1,0:T(8,128)(2,1)S(1)}, bf16[512,2048]{1,0:T(8,128)(2,1)}, u32[]{:S(2)}) copy-start(bf16[512,2048]{1,0:T(8,128)(2,1)} %param.29) | copy-start | bytes 6291460
  8.0 3.3 copy-start.7
  8.0 207.1 %all-gather.12.cloned.1.call-start = ((), (), s32[]{:S(2)}) async-start(), calls=%async_computation.6 | async-start | bytes 1310720 | tf_op jit(solution)/shard_map/all_gather | solution.py:24
  8.1 3.6 copy-start.2
  18.8 4.6 copy-start.5
  18.8 7.8 %copy-start.9 = (s32[1,16]{1,0:T(1,128)S(1)}, s32[1,16]{1,0:T(1,128)}, u32[]{:S(2)}) copy-start(s32[1,16]{1,0:T(1,128)} %param.35) | copy-start | bytes 196
  18.9 7.8 %copy-start.11 = (s32[1,16]{1,0:T(1,128)S(1)}, s32[1,16]{1,0:T(1,128)}, u32[]{:S(2)}) copy-start(s32[1,16]{1,0:T(1,128)} %param.34) | copy-start | bytes 196
  18.9 7.9 %copy-start.6 = (bf16[4,1024]{1,0:T(4,128)(2,1)S(1)}, bf16[4,1024]{1,0:T(4,128)(2,1)}, u32[]{:S(2)}) copy-start(bf16[4,1024]{1,0:T(4,128)(2,1)} %param.23) | copy-start | bytes 24580
  18.9 8.0 %copy-start.12 = (bf16[2048,16]{0,1:T(8,128)(2,1)S(1)}, bf16[2048,16]{0,1:T(8,128)(2,1)}, u32[]{:S(2)}) copy-start(bf16[2048,16]{0,1:T(8,128)(2,1)} %param.24) | copy-start | bytes 196612
  18.9 8.0 %copy-start.13 = (bf16[16,256]{1,0:T(8,128)(2,1)S(1)}, bf16[16,256]{1,0:T(8,128)(2,1)}, u32[]{:S(2)}) copy-start(bf16[16,256]{1,0:T(8,128)(2,1)} %param.25) | copy-start | bytes 24580
  18.9 7.9 %copy-start.14 = (f32[256]{0:T(256)S(1)}, f32[256]{0:T(256)}, u32[]{:S(2)}) copy-start(f32[256]{0:T(256)} %param.26) | copy-start | bytes 3076
  18.9 15.4 %collective-permute-start = (bf16[3,1024]{1,0:T(4,128)(2,1)S(1)}, bf16[3,1024]{1,0:T(4,128)(2,1)S(1)}, u32[]{:S(2)}, u32[]{:S(2)}) collective-permute-start(bf16[3,1024]{1,0:T(4,128)(2,1)S(1)} %slice_bitcast_fusion.2), channel_id=1, source_target_pairs={{0,2},{2,4},{4,6},{1,3},{3,5},{5,7},{8,10},{10,12},{12,14},{9,11},... | collective-permute-start | bytes 18440 | tf_op jit(solution)/shard_map/ppermute | solution.py:18
  31.7 1.0 copy-start.3
  41.7 1.6 copy-start.4
  45.4 144.7 %copy-start.10 = (bf16[512]{0:T(512)(128)(2,1)S(1)}, bf16[512]{0:T(512)(128)(2,1)}, u32[]{:S(2)}) copy-start(bf16[512]{0:T(512)(128)(2,1)} %param.28) | copy-start | bytes 3076
  189.5 80.8 %all-reduce.2.cloned.1.call-start = ((), (), s32[]{:S(2)}) async-start(), calls=%async_computation.1 | async-start | bytes 8388608 | tf_op jit(solution)/shard_map/psum | solution.py:193
  231.6 2.0 copy-start.8
  231.6 65.5 %all-gather.6.cloned.1.call-start = ((), (), s32[]{:S(2)}) async-start(), calls=%async_computation.2 | async-start | bytes 6127616 | tf_op jit(solution)/shard_map/all_gather | solution.py:201
  232.2 130.3 %all-gather.10.cloned.1.call-start = ((), (), s32[]{:S(2)}) async-start(), calls=%async_computation.4 | async-start | bytes 6127616 | tf_op jit(solution)/shard_map/all_gather | solution.py:206
  232.8 191.0 %all-gather.8.cloned.1.call-start = ((), (), s32[]{:S(2)}) async-start(), calls=%async_computation.3 | async-start | bytes 6127616 | tf_op jit(solution)/shard_map/all_gather | solution.py:202
  233.4 226.4 %reduce-scatter.2.cloned.1.call-start = ((), (), s32[]{:S(2)}) async-start(), calls=%async_computation.5 | async-start | bytes 6291456 | tf_op jit(solution)/shard_map/reduce_scatter | solution.py:209
  446.5 17.8 %copy-start.1 = (bf16[512,2048]{1,0:T(8,128)(2,1)S(1)}, bf16[512,2048]{1,0:T(8,128)(2,1)}, u32[]{:S(2)}) copy-start(bf16[512,2048]{1,0:T(8,128)(2,1)} %param.29) | copy-start | bytes 6291460
Sparse Core Ops, SparseCore 0:
  189.6 25.4 all-gather.11
  231.7 38.5 all-reduce.1
  444.8 14.9 reduce-scatter.1
Sparse Core Ops, SparseCore 1:
  234.4 62.6 all-gather.5
  299.3 63.2 all-gather.9
  364.7 59.0 all-gather.7
where the time goes:
time: 474 us; the launch traced here: 472 us
  waiting for transfers between devices  197 us (42%)
  matrix products  132 us (28%)
  local copies, waits for them, and re-layouts  77.3 us (16%)
  other arithmetic  36 us (8%)
  between operations  15.8 us (3%)
  blocking collectives  6.89 us (1%)
  starting transfers between devices  4.97 us (1%)
    dynamic_slice x80, local copies, waits for them, and re-layouts, on_device(): lax.scan(page_step, start_memory, (query_rows, key_rows, value_matrix, de...  70.5 us
    all_gather x1, waiting for transfers between devices, on_device(): up_part = widen(lax.all_gather(up_weight, 'req', axis=0, tiled=True))  61.3 us
    all_gather x1, waiting for transfers between devices, on_device(): lax.all_gather(down_weight, 'req', axis=1, tiled=True)  53.5 us
    psum x1, waiting for transfers between devices, on_device(): lax.psum(partial_value.astype(jnp.bfloat16), 'hid').astype(jnp.float32)  36.6 us
    dot_general x16, matrix products, page_step(): jnp.einsum('lte,ltb->leb', weighted_rows, value_matrix, precision=TOP_PRE...  35.4 us
    dot_general x16, matrix products, page_step(): jnp.einsum('eow,ews->eos', raised_rows, memory_state, precision=TOP_PRECI...  29 us
    dot_general x1, matrix products, on_device(): jnp.dot(hidden, lax.all_gather(down_weight, 'req', axis=1, tiled=True), p...  20.9 us
    all_gather x1, waiting for transfers between devices, on_device(): gate_part = widen(lax.all_gather(gate_weight, 'req', axis=0, tiled=True))  19.1 us
  transfers between devices with their start and end apart: 7, of which 6 were waited for; matrix products, arithmetic and copies ran while one was open for 8% of the time, Pallas kernels for 0%

commit v1 on v0

--- a/solution.py
+++ b/solution.py
@@ -10,6 +10,11 @@
 CONVW = 1024
 EPSILON = 1e-06
 TOP_PRECISION = lax.Precision.HIGHEST
+
+
+def summed_here(x, mesh_axis):
+    pieces = lax.all_gather(x, mesh_axis)
+    return jnp.sum(pieces, axis=0)
 
 
 def shifted(value, axis, steps):
@@ -190,7 +195,7 @@
     partial_value = jnp.dot(gated_rows, output_weight, preferred_element_type=jnp.float32)
     half_rows = token_count // lax.axis_size("hid")
     row_start = lax.axis_index("hid") * half_rows
-    mixed_sum = lax.psum(partial_value.astype(jnp.bfloat16), "hid").astype(jnp.float32)
+    mixed_sum = summed_here(partial_value.astype(jnp.bfloat16), "hid").astype(jnp.float32)
     residual = (tokens.astype(jnp.float32) + mixed_sum).astype(jnp.bfloat16)
     feed_in = rms_scaled(residual, mixer_gain).astype(jnp.bfloat16)
     own_residual = lax.dynamic_slice_in_dim(residual, row_start, half_rows, 0)

time: 474 us -> 497 us (1.049)
  waiting for transfers between devices: 197 us -> 213 us
  other arithmetic: 36 us -> 44.6 us
    psum x1 -> x0, waiting for transfers between devices: 36.6 us -> none  [on_device(): lax.psum(partial_value.astype(jnp.bfloat16), 'hid').astype(jnp.float32)]
    all_gather x1, waiting for transfers between devices: 19.1 us -> 45.5 us  [on_device(): gate_part = widen(lax.all_gather(gate_weight, 'req', axis=0, tiled=True))]
    all_gather x0 -> x1, waiting for transfers between devices: none -> 25.3 us  [summed_here(): pieces = lax.all_gather(x, mesh_axis)]
    all_gather x1, waiting for transfers between devices: 61.3 us -> 48.5 us  [on_device(): up_part = widen(lax.all_gather(up_weight, 'req', axis=0, tiled=True))]
    all_gather x1, waiting for transfers between devices: 53.5 us -> 65.9 us  [on_device(): lax.all_gather(down_weight, 'req', axis=1, tiled=True)]
    reduce_sum x0 -> x1, other arithmetic: none -> 8.78 us  [summed_here(): return jnp.sum(pieces, axis=0)]
  transfers between devices with their start and end apart: 7 -> 7, of which waited for: 6 -> 6; matrix products, arithmetic and copies ran while one was open for 8% -> 9% of each run, Pallas kernels for 0% -> 0%
where the time goes in v1:
time: 497 us; the launch traced here: 494 us
  waiting for transfers between devices  213 us (43%)
  matrix products  133 us (27%)
  local copies, waits for them, and re-layouts  77.3 us (16%)
  other arithmetic  44.6 us (9%)
  between operations  14.5 us (3%)
  blocking collectives  6.89 us (1%)
    dynamic_slice x80, local copies, waits for them, and re-layouts, on_device(): lax.scan(page_step, start_memory, (query_rows, key_rows, value_matrix, de...  70.5 us
    all_gather x1, waiting for transfers between devices, on_device(): lax.all_gather(down_weight, 'req', axis=1, tiled=True)  65.9 us
    all_gather x1, waiting for transfers between devices, on_device(): up_part = widen(lax.all_gather(up_weight, 'req', axis=0, tiled=True))  48.5 us
    all_gather x1, waiting for transfers between devices, on_device(): gate_part = widen(lax.all_gather(gate_weight, 'req', axis=0, tiled=True))  45.5 us
    dot_general x16, matrix products, page_step(): jnp.einsum('lte,ltb->leb', weighted_rows, value_matrix, precision=TOP_PRE...  35.4 us
    dot_general x16, matrix products, page_step(): jnp.einsum('eow,ews->eos', raised_rows, memory_state, precision=TOP_PRECI...  29 us
    all_gather x1, waiting for transfers between devices, summed_here(): pieces = lax.all_gather(x, mesh_axis)  25.3 us
    dot_general x1, matrix products, on_device(): jnp.dot(hidden, lax.all_gather(down_weight, 'req', axis=1, tiled=True), p...  20.9 us
  transfers between devices with their start and end apart: 7, of which 6 were waited for; matrix products, arithmetic and copies ran while one was open for 9% of the time, Pallas kernels for 0%

profile of v1, /device:TPU:1, one launch (start us, length us, event | category | flops | bytes accessed | tf_op | source)
XLA Modules:
  0.0 494.0 jit_solution(14421341568843880836)
XLA Ops:
  7.2 3.2 fusion.29
  10.8 7.2 %convolution_convert_fusion.2 = bf16[1024,1024]{1,0:T(8,128)(2,1)S(1)} fusion(bf16[2048,1024]{1,0:T(8,128)(2,1)} %param.22, bf16[1024,2048]{1,0:T(8,128)(2,1)S(1)} %copy-done.2, f32[2048]{0:T(1024)S(1)} %convert_element_type.148, f32[1024]{0:T(1024)S(1)} %add_rsqrt_fusion.2), kind=kOutput, calls=%fused_computation.78 | convolution fusion | flops 4304404480 | bytes 10498048 | tf_op jit(solution)/shard_map/dot_general | solution.py:141
  18.1 4.5 collective-permute-start
  22.6 3.2 copy_convert_fusion
  26.0 4.2 fusion.50
  33.6 7.3 %fusion.37 = f32[16,64,1,1024]{3,0,1,2:T(8,128)S(1)} fusion(f32[16,64,1024]{2,0,1:T(8,128)} %copy_convert_fusion, f32[16,3,1024]{2,0,1:T(8,128)S(1)} %convert_multiply_fusion.4, f32[1024]{0:T(1024)S(1)} %bitcast.170, f32[1024]{0:T(1024)S(1)} %bitcast.171, f32[1024]{0:T(1024)S(1)} %bitcast.169, f32[1024]{0:T(1024)S(1)} %bitcast.168), kind=kLoop, calls=%fused_computation.61 | loop fusion | flops 10485760 | bytes 8601600 | tf_op jit(solution)/shard_map/reshape | solution.py:147
  44.6 143.3 %while.28 = (s32[]{:T(128)}, f32[1,256,512]{2,1,0:T(8,128)S(1)}, f32[16,1,64,512]{3,2,1,0:T(8,128)}, f32[16,1,256,512]{3,2,1,0:T(8,128)}, f32[16,1,64,256]{3,0,1...) while((s32[]{:T(128)}, f32[1,256,512]{2,1,0:T(8,128)S(1)}, ...), condition=%wide.region_4.5_spmd.clone, body=%wide.region_3.4_spmd.clone.sunk | while | flops 240001024 | bytes 4038800 | solution.py:161
  69.2 2.2 bitcast_dynamic-update-slice_fusion.2
  190.0 6.9 %all_gather.25 = bf16[4,1,256]{2,1,0:T(2,128)(2,1)S(1)} all-gather(bf16[1,1,256]{2,1,0:T(2,128)(2,1)S(1)} %fusion.65), channel_id=1, replica_groups=mesh['req'=16,'seq'=4,'hid'=2] {'seq'}, dimensions={0}, use_global_device_ids=true | all-gather | bytes 2560 | tf_op jit(solution)/shard_map/all_gather | solution.py:29
  196.9 17.4 %all-gather.14.cloned.1.call-done = bf16[4,256,512]{2,1,0:T(8,128)(2,1)} async-done(((bf16[1,256,512]{2,1,0:T(8,128)(2,1)}), bf16[4,256,512]{2,1,0:T(8,128)(2,1)}) %all-gather.14.cloned.1.call-update) | async-done | bytes 1048592 | tf_op jit(solution)/shard_map/all_gather | solution.py:29
  214.5 5.6 %multiply_reduce_fusion = (f32[16,64]{1,0:T(8,128)S(1)}, f32[16,1,64,512]{3,2,0,1:T(8,128)}) fusion(f32[16,64,256]{2,0,1:T(8,128)} %get-tuple-element.223, f32[1,256,512]{2,1,0:T(8,128)S(1)} %get-tuple-element.98, f32[16,1,64,512]{3,2,1,0:T(8,128)} %get-tuple-element.96), kind=kOutput, calls=%fused_computation.77 | convolution fusion | flops 1612184576 | bytes 5771264 | tf_op jit(solution)/shard_map/dlof,lfg->dlog/dot_general | solution.py:181
  220.2 6.2 %fusion.44 = bf16[1024,512]{1,0:T(8,128)(2,1)S(1)} fusion(f32[16,1,64,512]{3,2,0,1:T(8,128)} %get-tuple-element.231, f32[512]{0:T(512)S(1)} %convert_element_type.165, f32[1024]{0:T(1024)S(1)} %rsqrt.29, bf16[2048,512]{1,0:T(8,128)(2,1)} %param.27, bf16[1024,2048]{1,0:T(8,128)(2,1)} %param.20, f32[2048]{0:T(1024)S(1)} %convert_element_type.148, ...), kind=kOutput, calls=%fused_computation.76 | convolution fusion | flops 2160066560 | bytes 9455616 | tf_op jit(solution)/shard_map/dot_general | solution.py:189
  226.4 4.4 convolution_convert_fusion.1
  232.7 25.3 %all-gather.16.cloned.1.call-done = bf16[2048,2048]{1,0:T(8,128)(2,1)} async-done(((bf16[1024,2048]{1,0:T(8,128)(2,1)}), bf16[2048,2048]{1,0:T(8,128)(2,1)}) %all-gather.16.cloned.1.call-update) | async-done | bytes 8388624 | tf_op jit(solution)/shard_map/all_gather | solution.py:16
  258.0 8.8 %reduce_sum.51 = bf16[1024,2048]{1,0:T(8,128)(2,1)} reduce(bf16[2,1024,2048]{2,1,0:T(8,128)(2,1)} %bitcast.157, bf16[]{:T(256)} %constant.97.clone.1), dimensions={0}, to_apply=%region_10.11 | reduce | flops 2097152 | bytes 12582914 | tf_op jit(solution)/shard_map/reduce_sum | solution.py:17
  266.8 7.5 %fusion.26 = (f32[1024]{0:T(1024)S(1)}, bf16[1024,2048]{1,0:T(8,128)(2,1)}) fusion(bf16[1024,2048]{1,0:T(8,128)(2,1)} %reduce_sum.51, bf16[1024,2048]{1,0:T(8,128)(2,1)} %param.20), kind=kLoop, calls=%fused_computation.44 | loop fusion | flops 14679040 | bytes 12587008 | tf_op jit(solution)/shard_map/reduce_sum | solution.py:50
  274.3 45.5 %all-gather.8.cloned.1.call-done = bf16[2048,1408]{1,0:T(8,128)(2,1)} async-done(((bf16[128,1408]{1,0:T(8,128)(2,1)}), bf16[2048,1408]{1,0:T(8,128)(2,1)}) %all-gather.8.cloned.1.call-update) | async-done | bytes 5767184 | tf_op jit(solution)/shard_map/all_gather | solution.py:206
  319.8 12.0 %fusion.47 = f32[1024,1408]{1,0:T(8,128)} fusion(bf16[2048,1408]{1,0:T(8,128)(2,1)} %all-gather.8.cloned.1.call-done, bf16[1024,2048]{1,0:T(8,128)(2,1)} %get-tuple-element.218, f32[2048]{0:T(1024)S(1)} %convert_element_type.172, f32[1024]{0:T(1024)S(1)} %add_rsqrt_fusion.1), kind=kOutput, calls=%fused_computation.81 | convolution fusion | flops 5913968640 | bytes 15740928 | tf_op jit(solution)/shard_map/dot_general | solution.py:204
  331.8 48.5 %all-gather.10.cloned.1.call-done = bf16[2048,1408]{1,0:T(8,128)(2,1)} async-done(((bf16[128,1408]{1,0:T(8,128)(2,1)}), bf16[2048,1408]{1,0:T(8,128)(2,1)}) %all-gather.10.cloned.1.call-update) | async-done | bytes 5767184 | tf_op jit(solution)/shard_map/all_gather | solution.py:207
  380.3 65.9 %all-gather.12.cloned.1.call-done = bf16[1408,2048]{1,0:T(8,128)(2,1)} async-done(((bf16[1408,128]{1,0:T(8,128)(2,1)}), bf16[1408,2048]{1,0:T(8,128)(2,1)}) %all-gather.12.cloned.1.call-update) | async-done | bytes 5767184 | tf_op jit(solution)/shard_map/all_gather | solution.py:211
  446.2 20.9 %convolution_convert_fusion = bf16[1024,2048]{1,0:T(8,128)(2,1)} fusion(bf16[1408,2048]{1,0:T(8,128)(2,1)} %all-gather.12.cloned.1.call-done, f32[1024,1408]{1,0:T(8,128)} %fusion.47, bf16[2048,1408]{1,0:T(8,128)(2,1)} %all-gather.10.cloned.1.call-done, bf16[1024,2048]{1,0:T(8,128)(2,1)} %get-tuple-element.218, f32[2048]{0:T(1024)S(1)} %convert_element_type.172, ...), kind=kOutput, calls=%fused_computation.68 | convolution fusion | flops 11830296576 | bytes 25702400 | tf_op jit(solution)/shard_map/dot_general | solution.py:209
  469.0 5.4 %add_convert_fusion = bf16[16,1,256,512]{3,2,1,0:T(8,128)(2,1)} fusion(f32[16,1,256,512]{3,2,1,0:T(8,128)} %get-tuple-element.99, f32[256,512]{1,0:T(8,128)S(1)} %bitcast.156, f32[16,256]{1,0:T(8,128)S(1)} %bitcast_multiply_fusion.1), kind=kLoop, calls=%fused_computation.51 | loop fusion | flops 6291456 | bytes 13123584 | tf_op jit(solution)/shard_map/convert_element_type | solution.py:218
  474.3 8.4 %reduce-scatter.2.cloned.1.call-done = bf16[512,2048]{1,0:T(8,128)(2,1)} async-done(((bf16[1024,2048]{1,0:T(8,128)(2,1)}), bf16[512,2048]{1,0:T(8,128)(2,1)}) %reduce-scatter.2.cloned.1.call-update) | async-done | bytes 2097168 | tf_op jit(solution)/shard_map/reduce_scatter | solution.py:214
  482.7 4.4 add_convert_fusion.1
  (257 shorter events, 154.1 us)
Async XLA Ops:
  7.2 219.2 %copy-start = (bf16[512,2048]{1,0:T(8,128)(2,1)S(1)}, bf16[512,2048]{1,0:T(8,128)(2,1)}, u32[]{:S(2)}) copy-start(bf16[512,2048]{1,0:T(8,128)(2,1)} %param.29) | copy-start | bytes 6291460
  7.2 3.3 copy-start.7
  7.2 207.1 %all-gather.14.cloned.1.call-start = ((), (), s32[]{:S(2)}) async-start(), calls=%async_computation.5 | async-start | bytes 1310720 | tf_op jit(solution)/shard_map/all_gather | solution.py:29
  7.2 3.6 copy-start.2
  18.0 4.6 copy-start.5
  18.0 7.8 %copy-start.9 = (s32[1,16]{1,0:T(1,128)S(1)}, s32[1,16]{1,0:T(1,128)}, u32[]{:S(2)}) copy-start(s32[1,16]{1,0:T(1,128)} %param.35) | copy-start | bytes 196
  18.0 7.8 %copy-start.11 = (s32[1,16]{1,0:T(1,128)S(1)}, s32[1,16]{1,0:T(1,128)}, u32[]{:S(2)}) copy-start(s32[1,16]{1,0:T(1,128)} %param.34) | copy-start | bytes 196
  18.0 7.9 %copy-start.6 = (bf16[4,1024]{1,0:T(4,128)(2,1)S(1)}, bf16[4,1024]{1,0:T(4,128)(2,1)}, u32[]{:S(2)}) copy-start(bf16[4,1024]{1,0:T(4,128)(2,1)} %param.23) | copy-start | bytes 24580
  18.1 7.9 %copy-start.12 = (bf16[2048,16]{0,1:T(8,128)(2,1)S(1)}, bf16[2048,16]{0,1:T(8,128)(2,1)}, u32[]{:S(2)}) copy-start(bf16[2048,16]{0,1:T(8,128)(2,1)} %param.24) | copy-start | bytes 196612
  18.1 7.9 %copy-start.13 = (bf16[16,256]{1,0:T(8,128)(2,1)S(1)}, bf16[16,256]{1,0:T(8,128)(2,1)}, u32[]{:S(2)}) copy-start(bf16[16,256]{1,0:T(8,128)(2,1)} %param.25) | copy-start | bytes 24580
  18.1 7.9 %copy-start.14 = (f32[256]{0:T(256)S(1)}, f32[256]{0:T(256)}, u32[]{:S(2)}) copy-start(f32[256]{0:T(256)} %param.26) | copy-start | bytes 3076
  18.1 15.4 %collective-permute-start = (bf16[3,1024]{1,0:T(4,128)(2,1)S(1)}, bf16[3,1024]{1,0:T(4,128)(2,1)S(1)}, u32[]{:S(2)}, u32[]{:S(2)}) collective-permute-start(bf16[3,1024]{1,0:T(4,128)(2,1)S(1)} %slice_bitcast_fusion.2), channel_id=1, source_target_pairs={{0,2},{2,4},{4,6},{1,3},{3,5},{5,7},{8,10},{10,12},{12,14},{9,11},... | collective-permute-start | bytes 18440 | tf_op jit(solution)/shard_map/ppermute | solution.py:23
  30.9 1.0 copy-start.3
  40.9 1.6 copy-start.4
  44.6 144.7 %copy-start.10 = (bf16[512]{0:T(512)(128)(2,1)S(1)}, bf16[512]{0:T(512)(128)(2,1)}, u32[]{:S(2)}) copy-start(bf16[512]{0:T(512)(128)(2,1)} %param.28) | copy-start | bytes 3076
  188.6 69.4 %all-gather.16.cloned.1.call-start = ((), (), s32[]{:S(2)}) async-start(), calls=%async_computation.6 | async-start | bytes 12582912 | tf_op jit(solution)/shard_map/all_gather | solution.py:16
  230.7 2.0 copy-start.8
  230.8 89.1 %all-gather.8.cloned.1.call-start = ((), (), s32[]{:S(2)}) async-start(), calls=%async_computation.1 | async-start | bytes 6127616 | tf_op jit(solution)/shard_map/all_gather | solution.py:206
  231.5 148.8 %all-gather.10.cloned.1.call-start = ((), (), s32[]{:S(2)}) async-start(), calls=%async_computation.2 | async-start | bytes 6127616 | tf_op jit(solution)/shard_map/all_gather | solution.py:207
  232.1 214.2 %all-gather.12.cloned.1.call-start = ((), (), s32[]{:S(2)}) async-start(), calls=%async_computation.3 | async-start | bytes 6127616 | tf_op jit(solution)/shard_map/all_gather | solution.py:211
  232.7 250.1 %reduce-scatter.2.cloned.1.call-start = ((), (), s32[]{:S(2)}) async-start(), calls=%async_computation.4 | async-start | bytes 6291456 | tf_op jit(solution)/shard_map/reduce_scatter | solution.py:214
  469.0 18.2 %copy-start.1 = (bf16[512,2048]{1,0:T(8,128)(2,1)S(1)}, bf16[512,2048]{1,0:T(8,128)(2,1)}, u32[]{:S(2)}) copy-start(bf16[512,2048]{1,0:T(8,128)(2,1)} %param.29) | copy-start | bytes 6291460
Sparse Core Ops, SparseCore 0:
  188.8 25.4 all-gather.13
  230.9 27.0 all-gather.15
  260.2 59.6 all-gather.7
  321.8 58.4 all-gather.9
  382.3 63.9 all-gather.11
  467.3 15.3 reduce-scatter.1
